TPU v7x, 512 devices: a whole 4x8x8 slice. The times are simulated.
512 devices in a mesh: row: 32 (over z, x), col: 16 (over y, core).
Axes of the slice: x: 4, y: 8, z: 8, core: 2. Of those that a mesh axis runs over, the one named last changes fastest.
Arguments:
- tiles: bfloat16 [32, 16, 32, 128, 128], P('row', 'col'), may hold values from -0.375 to 0.375
- coords: int32 [32, 16, 32, 2], P('row', 'col'), may hold values from 0 to 2047, as said below
- counts: int32 [32, 16], P('row', 'col'), may hold values from 16 to 32, as said below
- rhs: float32 [2, 4194304], P(None, ('row', 'col')), may hold values from -50 to 50
Outputs:
- solution: float32 [2, 4194304], P(None, ('col', 'row'))
- phi_bar: float32 [2], replicated
Inputs may be any that keep to these rules, and one draw needn't show every extreme that they name: coords[p, q, k, 0] is a local block row below 1024 and coords[p, q, k, 1] a local block column below 2048; within one tile no two slots share a block row and no two share a block column; counting all 32 slots of a tile, exactly 2 of its block rows fall in each of the 16 ranges of 64 consecutive block rows, and exactly 1 of its block columns in each of the 32 ranges of 64 consecutive block columns. The first counts[p, q] slots of tile (p, q) are used; some tile uses all 32.
All inputs are finite; a program needn't handle non-finite values.
Results may differ from a plain program's by a relative error of at most 0.015.
Values may be sent and summed in bfloat16 or wider, within the bound.
No kernel may reach another device: no remote copies, remote signals or barrier semaphores. Data moves between devices by JAX's collectives and lax.ppermute only.
A program may use at most 192 MiB of HBM per device.

v0:
```python
import jax
import jax.numpy as jnp
from jax import lax
from jax.sharding import PartitionSpec as P

ITERS = 2
EPS = 1e-06


def rounded(values):
    return lax.optimization_barrier(values.astype(jnp.bfloat16))


def select_blocks(piece, block_ids, block):
    width = piece.shape[1]
    offsets = block_ids[:, None] * block + jnp.arange(block, dtype=jnp.int32)[None, :]
    inside = (offsets >= 0) & (offsets < width)
    clipped = jnp.clip(offsets, 0, width - 1)
    taken = jnp.take(piece, clipped.reshape(-1), axis=1).reshape(
        piece.shape[0], block_ids.shape[0], block
    )
    taken = jnp.where(inside[None, :, :], taken, jnp.zeros_like(taken))
    values = piece.astype(jnp.float32)
    return (taken, jnp.sum(values * values, axis=1))


def forward_products(picked, tile_data):
    return jnp.einsum("rkc,kdc->krd", picked, tile_data, preferred_element_type=jnp.float32)


def adjoint_products(picked, tile_data):
    return jnp.einsum("rkd,kdc->krc", picked, tile_data, preferred_element_type=jnp.float32)


def bucket_blocks(products, block_ids, valid, range_len, owners):
    slot_count = block_ids.shape[0]
    capacity = slot_count // owners
    values = rounded(products * valid[:, None, None])
    owner_ids = block_ids // range_len
    local_ids = block_ids % range_len
    slot_index = jnp.arange(slot_count, dtype=jnp.int32)
    live = valid > 0.5
    earlier = (
        (owner_ids[:, None] == owner_ids[None, :])
        & live[None, :]
        & (slot_index[None, :] < slot_index[:, None])
    )
    position = jnp.sum(earlier.astype(jnp.int32), axis=1)
    target = owner_ids * capacity + position
    onehot = (target[None, :] == jnp.arange(owners * capacity, dtype=jnp.int32)[:, None]) & live[
        None, :
    ]
    sent = jnp.einsum(
        "ek,krd->erd", onehot.astype(jnp.bfloat16), values, preferred_element_type=jnp.float32
    ).astype(jnp.bfloat16)
    sent = sent.reshape(owners, capacity, values.shape[1], values.shape[2])
    labels = jnp.sum(jnp.where(onehot, local_ids[None, :] + 1, 0), axis=1).reshape(owners, capacity)
    return (sent, labels)


def place_blocks(received, labels, range_len):
    flat = received.reshape(-1, received.shape[2], received.shape[3])
    flat_labels = labels.reshape(-1)
    placing = (
        flat_labels[None, :] == jnp.arange(1, range_len + 1, dtype=jnp.int32)[:, None]
    ).astype(jnp.bfloat16)
    summed = jnp.einsum("bk,krd->rbd", placing, flat, preferred_element_type=jnp.float32)
    return summed.reshape(flat.shape[1], range_len * flat.shape[2])


def on_device(tiles, coords, counts, rhs):
    tile_data = tiles[0, 0]
    row_ids = coords[0, 0, :, 0]
    col_ids = coords[0, 0, :, 1]
    slot_count = tile_data.shape[0]
    block = tile_data.shape[1]
    valid = (jnp.arange(slot_count, dtype=jnp.int32) < counts[0, 0]).astype(jnp.float32)
    realizations = rhs.shape[0]
    piece_len = rhs.shape[1]
    range_len = piece_len // block

    def fold_rows(piece):
        return select_blocks(piece, row_ids, block)

    def fold_cols(piece):
        return select_blocks(piece, col_ids, block)

    def gather_u(u_rounded):
        return fold_rows(lax.all_gather(u_rounded, "col", axis=1, tiled=True))

    def gather_v(v_rounded):
        return fold_cols(lax.all_gather(v_rounded, "row", axis=1, tiled=True))

    def own_norm(vector_bf):
        values = vector_bf.astype(jnp.float32)
        return jnp.sqrt(lax.psum(jnp.sum(values * values, axis=1), ("row", "col")) + EPS)

    def u_norm(u_rounded):
        return own_norm(u_rounded)

    def v_norm(v_piece):
        return own_norm(v_piece)

    def forward_sum(picked_v):
        products = forward_products(picked_v, tile_data)
        sent, labels = bucket_blocks(products, row_ids, valid, range_len, lax.axis_size("col"))
        received, got_labels = (
            lax.all_to_all(sent, "col", split_axis=0, concat_axis=0, tiled=True),
            lax.all_to_all(labels, "col", split_axis=0, concat_axis=0, tiled=True),
        )
        return place_blocks(received, got_labels, range_len)

    def adjoint(picked_u, beta_now, v_former):
        products = adjoint_products(picked_u, tile_data)
        sent, labels = bucket_blocks(products, col_ids, valid, range_len, lax.axis_size("row"))
        received, got_labels = (
            lax.all_to_all(sent, "row", split_axis=0, concat_axis=0, tiled=True),
            lax.all_to_all(labels, "row", split_axis=0, concat_axis=0, tiled=True),
        )
        summed = place_blocks(received, got_labels, range_len)
        v_rounded = rounded(summed / beta_now[:, None] - beta_now[:, None] * v_former)
        picked_v, squares = gather_v(v_rounded)
        return (v_rounded, v_rounded, picked_v, squares)

    u_rounded = rounded(rhs)
    picked_u, u_squares = gather_u(u_rounded)
    beta_now = u_norm(u_rounded)
    u_unit = u_rounded.astype(jnp.float32) / beta_now[:, None]
    v_store, v_piece, picked_v, v_squares = adjoint(picked_u, beta_now, jnp.zeros((), jnp.float32))
    alpha_now = v_norm(v_piece)
    v_unit = v_store.astype(jnp.float32) / alpha_now[:, None]
    direction = v_piece.astype(jnp.float32) / alpha_now[:, None]
    solution = jnp.zeros((realizations, piece_len), jnp.float32)
    phi_bar = beta_now
    rho_bar = alpha_now
    for step in range(ITERS):
        final_turn = step + 1 == ITERS
        summed = forward_sum(picked_v)
        u_rounded = rounded(summed / alpha_now[:, None] - alpha_now[:, None] * u_unit)
        if final_turn:
            beta_now = u_norm(u_rounded)
        else:
            picked_u, u_squares = gather_u(u_rounded)
            beta_now = u_norm(u_rounded)
        rho_value = jnp.sqrt(rho_bar * rho_bar + beta_now * beta_now)
        cosine = rho_bar / rho_value
        sine = beta_now / rho_value
        phi_value = cosine * phi_bar
        phi_bar = sine * phi_bar
        solution = solution + (phi_value / rho_value)[:, None] * direction
        u_unit = u_rounded.astype(jnp.float32) / beta_now[:, None]
        if not final_turn:
            v_store, v_piece, picked_v, v_squares = adjoint(picked_u, beta_now, v_unit)
            alpha_now = v_norm(v_piece)
            theta_value = sine * alpha_now
            rho_bar = -cosine * alpha_now
            v_unit = v_store.astype(jnp.float32) / alpha_now[:, None]
            piece_unit = v_piece.astype(jnp.float32) / alpha_now[:, None]
            direction = piece_unit - (theta_value / rho_value)[:, None] * direction
    return (solution, phi_bar)


def solution(mesh):
    return jax.shard_map(
        on_device,
        mesh=mesh,
        in_specs=(
            P("row", "col", None, None, None),
            P("row", "col", None, None),
            P("row", "col"),
            P(None, ("row", "col")),
        ),
        out_specs=(P(None, ("col", "row")), P()),
        check_vma=False,
    )
```

profile of v0, /device:TPU:1, one launch (start us, length us, event | category | flops | bytes accessed | tf_op | source)
XLA Modules:
  0.0 923.0 jit_solution(12879823360342886995)
XLA Ops:
  7.9 0.7 fusion.82
  8.6 0.8 bitcast_multiply_fusion.1
  9.4 0.7 and_select_fusion.1
  10.4 0.7 copy.71
  11.1 13.7 %all-to-all-start.1 = ((s32[32,1,1]{2,1,0:T(1,128)}), s32[32,1,1]{2,1,0:T(1,128)S(1)}, u32[]{:S(2)}, u32[]{:S(2)}) async-start(s32[32,1,1]{2,1,0:T(1,128)} %copy.71), calls=%async_computation.1 | async-start | bytes 32768 | tf_op jit(solution)/shard_map/all_to_all | solution.py:118
  25.0 0.9 convert_element_type.88
  25.9 19.8 %all_gather.12 = bf16[2,131072]{1,0:T(2,128)(2,1)S(1)} all-gather(bf16[2,8192]{1,0:T(2,128)(2,1)S(1)} %convert_element_type.88), channel_id=1, replica_groups=mesh['row'=32,'col'=16] {'col'}, dimensions={1}, use_global_device_ids=true | all-gather | bytes 557056 | tf_op jit(solution)/shard_map/all_gather | solution.py:89
  45.8 20.3 %copy.66 = bf16[2,131072]{0,1:T(8,128)(2,1)} copy(bf16[2,131072]{1,0:T(2,128)(2,1)S(1)} %all_gather.12) | data formatting | bytes 1048576 | tf_op jit(solution)/shard_map/all_gather | solution.py:89
  66.2 43.7 %gather_fusion = bf16[4096,2]{1,0:T(8,128)(2,1)S(1)} fusion(bf16[2,131072]{0,1:T(8,128)(2,1)} %copy.66, s32[4096]{0:T(1024)S(1)} %fusion.37), kind=kCustom, calls=%fused_computation.clone | custom fusion | bytes 49152 | tf_op jit(solution)/shard_map/jit(_take)/gather | solution.py:19
  109.8 2.1 broadcast_select_fusion.3
  112.8 97.2 %psum.35 = f32[2]{0:T(128)S(1)} all-reduce(f32[2]{0:T(128)S(1)} %fusion.13), channel_id=1, replica_groups=mesh['row'=32,'col'=16] {'row','col'}, use_global_device_ids=true, to_apply=%region_3.5 | all-reduce | flops 2 | bytes 16 | tf_op jit(solution)/shard_map/psum | solution.py:96
  210.2 0.6 copy.69
  210.8 5.6 all-to-all-start
  216.4 0.7 reduce
  217.1 7.8 all-to-all-done
  225.1 0.7 fusion.18
  225.9 0.7 all_to_all.30
  226.6 6.4 all-to-all-start.3
  233.1 6.9 all-to-all-done.3
  240.5 0.7 reduce.4
  241.2 0.9 fusion.14
  242.2 94.6 %psum.36 = f32[2]{0:T(128)S(1)} all-reduce(f32[2]{0:T(128)S(1)} %fusion.14), channel_id=1, replica_groups=mesh['row'=32,'col'=16] {'row','col'}, use_global_device_ids=true, to_apply=%region_5.7 | all-reduce | flops 2 | bytes 16 | tf_op jit(solution)/shard_map/psum | solution.py:96
  336.8 40.2 %copy.72 = bf16[2,262144]{0,1:T(8,128)(2,1)} copy(bf16[2,262144]{1,0:T(2,128)(2,1)} %all-gather.3.cloned.1.call-done) | data formatting | bytes 2097152 | tf_op jit(solution)/shard_map/all_gather | solution.py:92
  377.0 43.7 %gather_fusion.1 = bf16[4096,2]{1,0:T(8,128)(2,1)S(1)} fusion(bf16[2,262144]{0,1:T(8,128)(2,1)} %copy.72, s32[4096]{0:T(1024)S(1)} %fusion.32), kind=kCustom, calls=%fused_computation.1.clone | custom fusion | bytes 49152 | tf_op jit(solution)/shard_map/jit(_take)/gather | solution.py:19
  420.7 2.1 broadcast_select_fusion.1
  423.2 0.7 fusion.1
  424.0 0.6 copy.75
  424.6 4.1 all-to-all-start.2
  428.7 7.3 all-to-all-done.2
  436.4 16.5 %all_gather.14 = bf16[2,131072]{1,0:T(2,128)(2,1)S(1)} all-gather(bf16[2,8192]{1,0:T(2,128)(2,1)S(1)} %fusion.19), channel_id=1, replica_groups=mesh['row'=32,'col'=16] {'col'}, dimensions={1}, use_global_device_ids=true | all-gather | bytes 557056 | tf_op jit(solution)/shard_map/all_gather | solution.py:89
  453.1 20.3 %copy.78 = bf16[2,131072]{0,1:T(8,128)(2,1)} copy(bf16[2,131072]{1,0:T(2,128)(2,1)S(1)} %all_gather.14) | data formatting | bytes 1048576 | tf_op jit(solution)/shard_map/all_gather | solution.py:89
  473.4 43.7 %gather_fusion.2 = bf16[4096,2]{1,0:T(8,128)(2,1)S(1)} fusion(bf16[2,131072]{0,1:T(8,128)(2,1)} %copy.78, s32[4096]{0:T(1024)S(1)} %fusion.37), kind=kCustom, calls=%fused_computation.2.clone | custom fusion | bytes 49152 | tf_op jit(solution)/shard_map/jit(_take)/gather | solution.py:19
  517.1 2.1 broadcast_select_fusion.2
  520.2 0.6 copy.81
  520.8 4.8 all-to-all-start.4
  525.7 97.1 %psum.37 = f32[2]{0:T(128)S(1)} all-reduce(f32[2]{0:T(128)S(1)} %fusion.15), channel_id=1, replica_groups=mesh['row'=32,'col'=16] {'row','col'}, use_global_device_ids=true, to_apply=%region_9.12 | all-reduce | flops 2 | bytes 16 | tf_op jit(solution)/shard_map/psum | solution.py:96
  623.1 0.7 fusion.21
  623.9 1.0 fusion.16
  624.8 94.9 %psum.38 = f32[2]{0:T(128)S(1)} all-reduce(f32[2]{0:T(128)S(1)} %fusion.16), channel_id=1, replica_groups=mesh['row'=32,'col'=16] {'row','col'}, use_global_device_ids=true, to_apply=%region_11.14 | all-reduce | flops 2 | bytes 16 | tf_op jit(solution)/shard_map/psum | solution.py:96
  719.7 40.2 %copy.83 = bf16[2,262144]{0,1:T(8,128)(2,1)} copy(bf16[2,262144]{1,0:T(2,128)(2,1)} %all-gather.5.cloned.1.call-done) | data formatting | bytes 2097152 | tf_op jit(solution)/shard_map/all_gather | solution.py:92
  759.9 43.7 %gather_fusion.3 = bf16[4096,2]{1,0:T(8,128)(2,1)S(1)} fusion(bf16[2,262144]{0,1:T(8,128)(2,1)} %copy.83, s32[4096]{0:T(1024)S(1)} %fusion.32), kind=kCustom, calls=%fused_computation.3.clone | custom fusion | bytes 49152 | tf_op jit(solution)/shard_map/jit(_take)/gather | solution.py:19
  803.6 2.1 broadcast_select_fusion
  806.1 0.7 fusion.3
  806.9 0.6 copy.86
  807.5 4.4 all-to-all-start.5
  811.9 7.3 all-to-all-done.5
  819.8 95.0 %psum.39 = f32[2]{0:T(128)S(1)} all-reduce(f32[2]{0:T(128)S(1)} %multiply_reduce_fusion), channel_id=1, replica_groups=mesh['row'=32,'col'=16] {'row','col'}, use_global_device_ids=true, to_apply=%region_13.16 | all-reduce | flops 2 | bytes 16 | tf_op jit(solution)/shard_map/psum | solution.py:96
  915.4 0.8 multiply_add_fusion
  (54 shorter events, 6.8 us)
Async XLA Ops:
  7.2 105.3 %copy-start = (bf16[1,1,32,128,128]{4,3,2,1,0:T(8,128)(2,1)S(1)}, bf16[1,1,32,128,128]{4,3,2,1,0:T(8,128)(2,1)}, u32[]{:S(2)}) copy-start(bf16[1,1,32,128,128]{4,3,2,1,0:T(8,128)(2,1)} %param.8) | copy-start | bytes 3145732
  11.1 199.7 %all-to-all-start.1 = ((s32[32,1,1]{2,1,0:T(1,128)}), s32[32,1,1]{2,1,0:T(1,128)S(1)}, u32[]{:S(2)}, u32[]{:S(2)}) async-start(s32[32,1,1]{2,1,0:T(1,128)} %copy.71), calls=%async_computation.1 | async-start | bytes 32768 | tf_op jit(solution)/shard_map/all_to_all | solution.py:118
  210.8 14.1 %all-to-all-start = ((bf16[32,1,2,128]{3,2,1,0:T(2,128)(2,1)}), bf16[32,1,2,128]{3,2,1,0:T(2,128)(2,1)S(1)}, u32[]{:S(2)}, u32[]{:S(2)}) async-start(bf16[32,1,2,128]{3,2,1,0:T(2,128)(2,1)} %copy.69), calls=%async_computation | async-start | bytes 32768 | tf_op jit(solution)/shard_map/all_to_all | solution.py:117
  216.4 120.5 %all-gather.3.cloned.1.call-start = ((), (), s32[]{:S(2)}) async-start(), calls=%async_computation.6 | async-start | bytes 1081344 | tf_op jit(solution)/shard_map/all_gather | solution.py:92
  225.9 397.2 %copy-start.1 = (bf16[2,8192]{1,0:T(2,128)(2,1)S(1)}, bf16[2,8192]{1,0:T(2,128)(2,1)}, u32[]{:S(2)}) copy-start(bf16[2,8192]{1,0:T(2,128)(2,1)} %fusion.18) | copy-start | bytes 98308
  226.6 13.4 %all-to-all-start.3 = ((s32[16,1,2]{2,1,0:T(1,128)}), s32[16,1,2]{2,1,0:T(1,128)S(1)}, u32[]{:S(2)}, u32[]{:S(2)}) async-start(s32[16,1,2]{2,1,0:T(1,128)} %bitcast.19), calls=%async_computation.3 | async-start | bytes 16384 | tf_op jit(solution)/shard_map/all_to_all | solution.py:109
  424.6 11.4 %all-to-all-start.2 = ((bf16[16,2,2,128]{3,1,2,0:T(2,128)(2,1)}), bf16[16,2,2,128]{3,1,2,0:T(2,128)(2,1)S(1)}, u32[]{:S(2)}, u32[]{:S(2)}) async-start(bf16[16,2,2,128]{3,1,2,0:T(2,128)(2,1)} %copy.75), calls=%async_computation.2 | async-start | bytes 32768 | tf_op jit(solution)/shard_map/all_to_all | solution.py:108
  520.8 102.0 %all-to-all-start.4 = ((bf16[32,1,2,128]{3,2,1,0:T(2,128)(2,1)}), bf16[32,1,2,128]{3,2,1,0:T(2,128)(2,1)S(1)}, u32[]{:S(2)}, u32[]{:S(2)}) async-start(bf16[32,1,2,128]{3,2,1,0:T(2,128)(2,1)} %copy.81), calls=%async_computation.4 | async-start | bytes 32768 | tf_op jit(solution)/shard_map/all_to_all | solution.py:117
  525.6 194.1 %all-gather.5.cloned.1.call-start = ((), (), s32[]{:S(2)}) async-start(), calls=%async_computation.7 | async-start | bytes 1081344 | tf_op jit(solution)/shard_map/all_gather | solution.py:92
  623.8 291.5 %copy-start.2 = (bf16[2,8192]{1,0:T(2,128)(2,1)S(1)}, bf16[2,8192]{1,0:T(2,128)(2,1)}, u32[]{:S(2)}) copy-start(bf16[2,8192]{1,0:T(2,128)(2,1)} %get-tuple-element.20) | copy-start | bytes 98308
  807.5 11.7 %all-to-all-start.5 = ((bf16[16,2,2,128]{3,1,2,0:T(2,128)(2,1)}), bf16[16,2,2,128]{3,1,2,0:T(2,128)(2,1)S(1)}, u32[]{:S(2)}, u32[]{:S(2)}) async-start(bf16[16,2,2,128]{3,1,2,0:T(2,128)(2,1)} %copy.86), calls=%async_computation.5 | async-start | bytes 32768 | tf_op jit(solution)/shard_map/all_to_all | solution.py:108
Sparse Core Ops, SparseCore 0:
  226.0 71.4 all-gather.2
  624.0 71.4 all-gather.4
where the time goes:
time: 929 us; the launch traced here: 923 us
  blocking collectives  515 us (55%)
  local copies, waits for them, and re-layouts  302 us (33%)
  starting transfers between devices  39 us (4%)
  waiting for transfers between devices  29.3 us (3%)
  other arithmetic  19.2 us (2%)
  between operations  15 us (2%)
    psum x5, blocking collectives, own_norm(): lax.psum(jnp.sum(values * values, axis=1), ('row', 'col')) + EPS  479 us
    gather x4, local copies, waits for them, and re-layouts, select_blocks(): jnp.take(piece, clipped.reshape(-1), axis=1)  175 us
    all_gather x2, local copies, waits for them, and re-layouts, gather_v(): return fold_cols(lax.all_gather(v_rounded, 'row', axis=1, tiled=True))  80.3 us
    all_gather x2, local copies, waits for them, and re-layouts, gather_u(): return fold_rows(lax.all_gather(u_rounded, 'col', axis=1, tiled=True))  40.6 us
    all_gather x2, blocking collectives, gather_u(): return fold_rows(lax.all_gather(u_rounded, 'col', axis=1, tiled=True))  36.3 us
  transfers between devices with their start and end apart: 8, of which 4 were waited for; matrix products, arithmetic and copies ran while one was open for 8% of the time, Pallas kernels for 0%

commit v1 on v0

--- a/solution.py
+++ b/solution.py
@@ -89,7 +89,17 @@
         return fold_rows(lax.all_gather(u_rounded, "col", axis=1, tiled=True))
 
     def gather_v(v_rounded):
-        return fold_cols(lax.all_gather(v_rounded, "row", axis=1, tiled=True))
+        return fold_cols(
+            jnp.concatenate(
+                jax.lax.all_to_all(
+                    jnp.stack([v_rounded for _ in range(jax.lax.axis_size("row"))]),
+                    "row",
+                    concat_axis=0,
+                    split_axis=0,
+                ),
+                axis=1,
+            )
+        )
 
     def own_norm(vector_bf):
         values = vector_bf.astype(jnp.float32)

time: 929 us -> 960 us (1.033)
  blocking collectives: 515 us -> 551 us
  between operations: 15 us -> 1.64 us
  starting transfers between devices: 39 us -> 51.1 us
    all_gather x2 -> x0, local copies, waits for them, and re-layouts: 80.3 us -> none  [gather_v(): return fold_cols(lax.all_gather(v_rounded, 'row', axis=1, tiled=True))]
    reshape x0 -> x2, local copies, waits for them, and re-layouts: none -> 80.3 us  [gather_v(): jnp.concatenate(jax.lax.all_to_all(jnp.stack([v_rounded for _ in range(ja...]
    psum x5, blocking collectives: 479 us -> 515 us  [own_norm(): lax.psum(jnp.sum(values * values, axis=1), ('row', 'col')) + EPS]
    all_to_all x0 -> x2, starting transfers between devices: none -> 9.65 us  [gather_v(): jax.lax.all_to_all(jnp.stack([v_rounded for _ in range(jax.lax.axis_size(...]
  transfers between devices with their start and end apart: 8 -> 8, of which waited for: 4 -> 4; matrix products, arithmetic and copies ran while one was open for 8% -> 7% of each run, Pallas kernels for 0% -> 0%
where the time goes in v1:
time: 960 us; the launch traced here: 958 us
  blocking collectives  551 us (57%)
  local copies, waits for them, and re-layouts  305 us (32%)
  starting transfers between devices  51.1 us (5%)
  waiting for transfers between devices  28.6 us (3%)
  other arithmetic  16.4 us (2%)
    psum x5, blocking collectives, own_norm(): lax.psum(jnp.sum(values * values, axis=1), ('row', 'col')) + EPS  515 us
    gather x4, local copies, waits for them, and re-layouts, select_blocks(): jnp.take(piece, clipped.reshape(-1), axis=1)  175 us
    reshape x2, local copies, waits for them, and re-layouts, gather_v(): jnp.concatenate(jax.lax.all_to_all(jnp.stack([v_rounded for _ in range(ja...  80.3 us
    all_gather x2, local copies, waits for them, and re-layouts, gather_u(): return fold_rows(lax.all_gather(u_rounded, 'col', axis=1, tiled=True))  40.6 us
    all_gather x2, blocking collectives, gather_u(): return fold_rows(lax.all_gather(u_rounded, 'col', axis=1, tiled=True))  36.3 us
  transfers between devices with their start and end apart: 8, of which 4 were waited for; matrix products, arithmetic and copies ran while one was open for 7% of the time, Pallas kernels for 0%

profile of v1, /device:TPU:1, one launch (start us, length us, event | category | flops | bytes accessed | tf_op | source)
XLA Modules:
  0.0 957.8 jit_solution(5591673812600939221)
XLA Ops:
  1.4 0.7 fusion.82
  2.1 0.8 bitcast_multiply_fusion.1
  2.9 0.7 and_select_fusion.1
  3.9 0.7 copy.79
  4.6 13.7 %all-to-all-start.1 = ((s32[32,1,1]{2,1,0:T(1,128)}), s32[32,1,1]{2,1,0:T(1,128)S(1)}, u32[]{:S(2)}, u32[]{:S(2)}) async-start(s32[32,1,1]{2,1,0:T(1,128)} %copy.79), calls=%async_computation.1 | async-start | bytes 32768 | tf_op jit(solution)/shard_map/all_to_all | solution.py:128
  18.4 0.9 convert_element_type.88
  19.3 19.8 %all_gather.6 = bf16[2,131072]{1,0:T(2,128)(2,1)S(1)} all-gather(bf16[2,8192]{1,0:T(2,128)(2,1)S(1)} %convert_element_type.88), channel_id=1, replica_groups=mesh['row'=32,'col'=16] {'col'}, dimensions={1}, use_global_device_ids=true | all-gather | bytes 557056 | tf_op jit(solution)/shard_map/all_gather | solution.py:89
  39.3 20.3 %copy.74 = bf16[2,131072]{0,1:T(8,128)(2,1)} copy(bf16[2,131072]{1,0:T(2,128)(2,1)S(1)} %all_gather.6) | data formatting | bytes 1048576 | tf_op jit(solution)/shard_map/all_gather | solution.py:89
  59.6 43.7 %gather_fusion = bf16[4096,2]{1,0:T(8,128)(2,1)S(1)} fusion(bf16[2,131072]{0,1:T(8,128)(2,1)} %copy.74, s32[4096]{0:T(1024)S(1)} %fusion.37), kind=kCustom, calls=%fused_computation.clone | custom fusion | bytes 49152 | tf_op jit(solution)/shard_map/jit(_take)/gather | solution.py:19
  103.3 2.1 broadcast_select_fusion.3
  106.3 97.2 %psum.35 = f32[2]{0:T(128)S(1)} all-reduce(f32[2]{0:T(128)S(1)} %fusion.13), channel_id=1, replica_groups=mesh['row'=32,'col'=16] {'row','col'}, use_global_device_ids=true, to_apply=%region_3.5 | all-reduce | flops 2 | bytes 16 | tf_op jit(solution)/shard_map/psum | solution.py:106
  203.6 0.6 copy.77
  204.2 5.6 all-to-all-start
  209.8 0.7 all_to_all.37
  210.5 0.7 reduce
  211.2 7.2 all-to-all-done
  218.3 6.4 all-to-all-start.4
  225.1 6.6 all-to-all-done.4
  231.7 1.9 stack.4
  233.7 3.9 all-to-all-start.2
  238.3 0.7 reduce.4
  239.2 111.7 %psum.36 = f32[2]{0:T(128)S(1)} all-reduce(f32[2]{0:T(128)S(1)} %fusion.14), channel_id=1, replica_groups=mesh['row'=32,'col'=16] {'row','col'}, use_global_device_ids=true, to_apply=%region_5.7 | all-reduce | flops 2 | bytes 16 | tf_op jit(solution)/shard_map/psum | solution.py:106
  350.9 40.2 %copy.80 = bf16[2,32,8192]{0,2,1:T(8,128)(2,1)} copy(bf16[2,32,8192]{2,0,1:T(2,128)(2,1)S(1)} %bitcast.143) | data formatting | bytes 2097152 | tf_op jit(solution)/shard_map/reshape | solution.py:93
  391.1 43.7 %gather_fusion.1 = bf16[4096,2]{1,0:T(8,128)(2,1)S(1)} fusion(bf16[2,262144]{0,1:T(8,128)(2,1)} %bitcast.16, s32[4096]{0:T(1024)S(1)} %fusion.32), kind=kCustom, calls=%fused_computation.1.clone | custom fusion | bytes 49152 | tf_op jit(solution)/shard_map/jit(_take)/gather | solution.py:19
  434.8 2.1 broadcast_select_fusion.1
  437.3 0.7 fusion.1
  438.1 0.6 copy.83
  438.7 4.3 all-to-all-start.3
  443.0 7.4 all-to-all-done.3
  450.9 16.5 %all_gather.7 = bf16[2,131072]{1,0:T(2,128)(2,1)S(1)} all-gather(bf16[2,8192]{1,0:T(2,128)(2,1)S(1)} %fusion.19), channel_id=1, replica_groups=mesh['row'=32,'col'=16] {'col'}, dimensions={1}, use_global_device_ids=true | all-gather | bytes 557056 | tf_op jit(solution)/shard_map/all_gather | solution.py:89
  467.5 20.3 %copy.86 = bf16[2,131072]{0,1:T(8,128)(2,1)} copy(bf16[2,131072]{1,0:T(2,128)(2,1)S(1)} %all_gather.7) | data formatting | bytes 1048576 | tf_op jit(solution)/shard_map/all_gather | solution.py:89
  487.9 43.7 %gather_fusion.2 = bf16[4096,2]{1,0:T(8,128)(2,1)S(1)} fusion(bf16[2,131072]{0,1:T(8,128)(2,1)} %copy.86, s32[4096]{0:T(1024)S(1)} %fusion.37), kind=kCustom, calls=%fused_computation.2.clone | custom fusion | bytes 49152 | tf_op jit(solution)/shard_map/jit(_take)/gather | solution.py:19
  531.5 2.1 broadcast_select_fusion.2
  534.6 0.6 copy.89
  535.2 7.5 all-to-all-start.5
  542.8 97.1 %psum.37 = f32[2]{0:T(128)S(1)} all-reduce(f32[2]{0:T(128)S(1)} %fusion.15), channel_id=1, replica_groups=mesh['row'=32,'col'=16] {'row','col'}, use_global_device_ids=true, to_apply=%region_9.12 | all-reduce | flops 2 | bytes 16 | tf_op jit(solution)/shard_map/psum | solution.py:106
  640.3 1.9 stack.5
  642.2 5.7 all-to-all-start.6
  648.2 113.2 %psum.38 = f32[2]{0:T(128)S(1)} all-reduce(f32[2]{0:T(128)S(1)} %fusion.16), channel_id=1, replica_groups=mesh['row'=32,'col'=16] {'row','col'}, use_global_device_ids=true, to_apply=%region_11.14 | all-reduce | flops 2 | bytes 16 | tf_op jit(solution)/shard_map/psum | solution.py:106
  761.4 40.2 %copy.91 = bf16[2,32,8192]{0,2,1:T(8,128)(2,1)} copy(bf16[2,32,8192]{2,0,1:T(2,128)(2,1)S(1)} %bitcast.144) | data formatting | bytes 2097152 | tf_op jit(solution)/shard_map/reshape | solution.py:93
  801.6 43.7 %gather_fusion.3 = bf16[4096,2]{1,0:T(8,128)(2,1)S(1)} fusion(bf16[2,262144]{0,1:T(8,128)(2,1)} %bitcast.30, s32[4096]{0:T(1024)S(1)} %fusion.32), kind=kCustom, calls=%fused_computation.3.clone | custom fusion | bytes 49152 | tf_op jit(solution)/shard_map/jit(_take)/gather | solution.py:19
  845.2 2.1 broadcast_select_fusion
  847.8 0.7 fusion.3
  848.6 0.6 copy.94
  849.2 4.0 all-to-all-start.7
  853.2 7.4 all-to-all-done.7
  861.2 95.3 %psum.39 = f32[2]{0:T(128)S(1)} all-reduce(f32[2]{0:T(128)S(1)} %multiply_reduce_fusion), channel_id=1, replica_groups=mesh['row'=32,'col'=16] {'row','col'}, use_global_device_ids=true, to_apply=%region_13.16 | all-reduce | flops 2 | bytes 16 | tf_op jit(solution)/shard_map/psum | solution.py:106
  957.1 0.8 multiply_add_fusion
  (50 shorter events, 7.3 us)
Async XLA Ops:
  0.6 105.3 %copy-start = (bf16[1,1,32,128,128]{4,3,2,1,0:T(8,128)(2,1)S(1)}, bf16[1,1,32,128,128]{4,3,2,1,0:T(8,128)(2,1)}, u32[]{:S(2)}) copy-start(bf16[1,1,32,128,128]{4,3,2,1,0:T(8,128)(2,1)} %param.8) | copy-start | bytes 3145732
  4.6 199.7 %all-to-all-start.1 = ((s32[32,1,1]{2,1,0:T(1,128)}), s32[32,1,1]{2,1,0:T(1,128)S(1)}, u32[]{:S(2)}, u32[]{:S(2)}) async-start(s32[32,1,1]{2,1,0:T(1,128)} %copy.79), calls=%async_computation.1 | async-start | bytes 32768 | tf_op jit(solution)/shard_map/all_to_all | solution.py:128
  204.2 14.1 %all-to-all-start = ((bf16[32,1,2,128]{3,2,1,0:T(2,128)(2,1)}), bf16[32,1,2,128]{3,2,1,0:T(2,128)(2,1)S(1)}, u32[]{:S(2)}, u32[]{:S(2)}) async-start(bf16[32,1,2,128]{3,2,1,0:T(2,128)(2,1)} %copy.77), calls=%async_computation | async-start | bytes 32768 | tf_op jit(solution)/shard_map/all_to_all | solution.py:127
  218.3 13.4 %all-to-all-start.4 = ((s32[16,1,2]{2,1,0:T(1,128)}), s32[16,1,2]{2,1,0:T(1,128)S(1)}, u32[]{:S(2)}, u32[]{:S(2)}) async-start(s32[16,1,2]{2,1,0:T(1,128)} %bitcast.21), calls=%async_computation.4 | async-start | bytes 16384 | tf_op jit(solution)/shard_map/all_to_all | solution.py:119
  233.7 117.3 %all-to-all-start.2 = ((bf16[32,2,8192]{2,1,0:T(2,128)(2,1)}), bf16[32,2,8192]{2,1,0:T(2,128)(2,1)S(1)}, u32[]{:S(2)}, u32[]{:S(2)}) async-start(bf16[32,2,8192]{2,1,0:T(2,128)(2,1)} %stack.4), calls=%async_computation.2 | async-start | bytes 2097152 | tf_op jit(solution)/shard_map/all_to_all | solution.py:94
  438.7 11.7 %all-to-all-start.3 = ((bf16[16,2,2,128]{3,1,2,0:T(2,128)(2,1)}), bf16[16,2,2,128]{3,1,2,0:T(2,128)(2,1)S(1)}, u32[]{:S(2)}, u32[]{:S(2)}) async-start(bf16[16,2,2,128]{3,1,2,0:T(2,128)(2,1)} %copy.83), calls=%async_computation.3 | async-start | bytes 32768 | tf_op jit(solution)/shard_map/all_to_all | solution.py:118
  535.2 104.7 %all-to-all-start.5 = ((bf16[32,1,2,128]{3,2,1,0:T(2,128)(2,1)}), bf16[32,1,2,128]{3,2,1,0:T(2,128)(2,1)S(1)}, u32[]{:S(2)}, u32[]{:S(2)}) async-start(bf16[32,1,2,128]{3,2,1,0:T(2,128)(2,1)} %copy.89), calls=%async_computation.5 | async-start | bytes 32768 | tf_op jit(solution)/shard_map/all_to_all | solution.py:127
  642.2 119.1 %all-to-all-start.6 = ((bf16[32,2,8192]{2,1,0:T(2,128)(2,1)}), bf16[32,2,8192]{2,1,0:T(2,128)(2,1)S(1)}, u32[]{:S(2)}, u32[]{:S(2)}) async-start(bf16[32,2,8192]{2,1,0:T(2,128)(2,1)} %stack.5), calls=%async_computation.6 | async-start | bytes 2097152 | tf_op jit(solution)/shard_map/all_to_all | solution.py:94
  849.2 11.4 %all-to-all-start.7 = ((bf16[16,2,2,128]{3,1,2,0:T(2,128)(2,1)}), bf16[16,2,2,128]{3,1,2,0:T(2,128)(2,1)S(1)}, u32[]{:S(2)}, u32[]{:S(2)}) async-start(bf16[16,2,2,128]{3,1,2,0:T(2,128)(2,1)} %copy.94), calls=%async_computation.7 | async-start | bytes 32768 | tf_op jit(solution)/shard_map/all_to_all | solution.py:118
